TPU v7x, 512 devices: a whole 4x4x16 slice. The times are simulated.
512 devices in a mesh: ctx: 64 (over y_hi, z, core), dp: 8 (over x, y_lo).
Axes of the slice: x: 4, y: 4 (y_hi: 2, y_lo: 2; y = y_hi * 2 + y_lo), z: 16, core: 2. Of those that a mesh axis runs over, the one named last changes fastest.
Arguments:
- queries: bfloat16 [8192, 2048], P('ctx', 'dp')
- keys: bfloat16 [8192, 2048], P('ctx', 'dp')
- values: bfloat16 [8192, 2048], P('ctx', 'dp'), may hold values from -6 to 6
- old_keys: bfloat16 [2048, 2048], P('ctx', 'dp'), may hold values from -6 to 6
- old_values: bfloat16 [2048, 2048], P('ctx', 'dp'), may hold values from -6 to 6
- conv_keys: bfloat16 [16, 4, 128, 128], P('dp'), may hold values from -0.25 to 0.25
- conv_values: bfloat16 [16, 4, 128, 128], P('dp'), may hold values from -0.25 to 0.25
- out_proj: bfloat16 [4096, 2048], P('ctx', 'dp'), may hold values from -0.125 to 0.125
- residual: bfloat16 [8192, 4096], P('ctx', 'dp'), may hold values from -4 to 4
- gain: bfloat16 [4096], P('dp'), may hold values from 0.5 to 1.5
- span_order: int32 [128], P('ctx'), may hold values from 0 to 127, as said below
- memory_length: int32 [1], replicated, may hold values from 128 to 512
Outputs:
- layer_out: bfloat16 [8192, 4096], P('ctx', 'dp')
Inputs may be any that keep to these rules, and one draw needn't show every extreme that they name: `span_order`: entries 2 i and 2 i + 1 are blocks c and 127 - c for some c, in either order; every block appears once. `memory_length`: the valid slots are the last ones.
All inputs are finite; a program needn't handle non-finite values.
Results may differ from a plain program's by a relative error of at most 0.018.
Values may be sent and summed in bfloat16 or wider, within the bound.
A program may use at most 64 MiB of HBM per device.

v0:
```python
import math
import jax
import jax.numpy as jnp
from jax import lax
from jax.sharding import PartitionSpec as P

neg_big = -1e30


def compress(old, conv_weight):
    slots = old.shape[0] // 4
    groups = conv_weight.shape[0]
    width = conv_weight.shape[2]
    grouped = old.reshape(slots, 4, groups, width)
    mixed = jnp.einsum("jthc,htce->jhe", grouped, conv_weight, preferred_element_type=jnp.float32)
    return mixed.reshape(slots, groups * width).astype(jnp.bfloat16)


def attend(carry, queries3, key_rows, value_rows, allowed, scale):
    run_max, run_sum, run_acc = carry
    rows = key_rows.shape[0]
    groups = queries3.shape[1]
    width = queries3.shape[2]
    keys3 = key_rows.reshape(rows, groups, width)
    values3 = value_rows.reshape(rows, groups, width)
    scores = jnp.einsum("thd,rhd->htr", queries3, keys3, preferred_element_type=jnp.float32) * scale
    scores = jnp.where(allowed[None], scores, neg_big)
    new_max = jnp.maximum(run_max, jnp.max(scores, axis=2))
    weights = jnp.where(allowed[None], jnp.exp(scores - new_max[:, :, None]), 0.0)
    factor = jnp.exp(run_max - new_max)
    new_sum = run_sum * factor + jnp.sum(weights, axis=2)
    update = jnp.einsum(
        "htr,rhd->htd", weights.astype(jnp.bfloat16), values3, preferred_element_type=jnp.float32
    )
    return (new_max, new_sum, run_acc * factor[:, :, None] + update)


def local(
    queries,
    keys,
    values,
    old_keys,
    old_values,
    conv_keys,
    conv_values,
    out_proj,
    residual,
    gain,
    span_order,
    memory_length,
):
    tok_rows = queries.shape[0]
    groups = conv_keys.shape[0]
    width = conv_keys.shape[2]
    half_rows = tok_rows // 2
    scale = 1.0 / math.sqrt(width)
    ctx_count = lax.axis_size("ctx")
    gain_f = gain.astype(jnp.float32)[None, :]
    offsets = jnp.arange(half_rows, dtype=jnp.int32)
    query_pos = (span_order[:, None] * half_rows + offsets[None, :]).reshape(tok_rows)
    queries3 = queries.reshape(tok_rows, groups, width)
    table = lax.all_gather(span_order, "ctx", axis=0, tiled=True)
    slot_count = old_keys.shape[0] // 4 * ctx_count
    first_valid = slot_count - memory_length[0]
    start_carry = (
        jnp.full((groups, tok_rows), neg_big, jnp.float32),
        jnp.zeros((groups, tok_rows), jnp.float32),
        jnp.zeros((groups, tok_rows, width), jnp.float32),
    )
    whole_keys, whole_values = (
        lax.all_gather(old_keys, "ctx", axis=0, tiled=True),
        lax.all_gather(old_values, "ctx", axis=0, tiled=True),
    )
    mem_keys = compress(whole_keys, conv_keys)
    mem_values = compress(whole_values, conv_values)
    slot_index = jnp.arange(slot_count, dtype=jnp.int32)
    visible = jnp.broadcast_to((slot_index >= first_valid)[None, :], (tok_rows, slot_count))
    carry = attend(start_carry, queries3, mem_keys, mem_values, visible, scale)
    span_ids = jnp.arange(table.shape[0], dtype=jnp.int32)
    pieces = (
        lax.all_gather(keys, "ctx", axis=0, tiled=True),
        lax.all_gather(values, "ctx", axis=0, tiled=True),
    )
    rows = pieces[0].shape[0]
    index = jnp.arange(rows, dtype=jnp.int32)
    slot_span = index // half_rows
    picked = jnp.sum(jnp.where(slot_span[:, None] == span_ids[None, :], table[None, :], 0), axis=1)
    key_pos = picked * half_rows + index % half_rows
    visible = key_pos[None, :] <= query_pos[:, None]
    run_max, run_sum, run_acc = attend(carry, queries3, pieces[0], pieces[1], visible, scale)
    attn = (
        (run_acc / run_sum[:, :, None])
        .transpose(1, 0, 2)
        .reshape(tok_rows, groups * width)
        .astype(jnp.bfloat16)
    )
    partial_sums = lax.dot_general(
        attn,
        lax.all_gather(out_proj, "ctx", axis=0, tiled=True),
        (((1,), (1,)), ((), ())),
        preferred_element_type=jnp.float32,
    )
    features = partial_sums.shape[1]
    share = lax.psum_scatter(
        partial_sums.astype(jnp.bfloat16), "dp", scatter_dimension=1, tiled=True
    ).astype(jnp.float32)
    stream = residual.astype(jnp.float32) + share
    power = lax.psum(jnp.sum(stream * stream, axis=1), "dp") / features
    normed = stream * lax.rsqrt(power + 1e-06)[:, None] * gain_f
    return normed.astype(jnp.bfloat16)


def solution(mesh):
    placed = (
        P("ctx", "dp"),
        P("ctx", "dp"),
        P("ctx", "dp"),
        P("ctx", "dp"),
        P("ctx", "dp"),
        P("dp", None, None, None),
        P("dp", None, None, None),
        P("ctx", "dp"),
        P("ctx", "dp"),
        P("dp"),
        P("ctx"),
        P(),
    )
    return jax.shard_map(
        local, mesh=mesh, in_specs=placed, out_specs=P("ctx", "dp"), check_vma=False
    )
```

profile of v0, /device:TPU:16, one launch (start us, length us, event | category | flops | bytes accessed | tf_op | source)
XLA Modules:
  0.0 803.5 jit_solution(13249138557412104678)
XLA Ops:
  6.5 0.0 copy-start
  6.5 0.0 copy-start.4
  6.5 0.0 all-gather.6.cloned.1.call-start
  6.5 0.7 all-gather.6.cloned.1.call-update
  7.3 0.0 all-gather.8.cloned.1.call-start
  7.3 0.7 all-gather.8.cloned.1.call-update
  8.0 0.0 all-gather.12.cloned.1.call-start
  8.1 0.7 all-gather.12.cloned.1.call-update
  8.7 0.0 all-gather.10.cloned.1.call-start
  8.8 1.6 copy.39
  10.4 0.0 all-gather.10.cloned.1.call-update
  10.4 0.0 all-gather.14.cloned.1.call-start
  10.4 0.5 all-gather.14.cloned.1.call-update
  11.0 0.0 reduce-scatter.2.cloned.1.call-start
  11.0 0.7 broadcast_multiply_fusion
  11.7 1.3 dynamic-slice
  13.6 0.9 dynamic-update-slice
  14.5 28.8 %all-reduce = s32[128]{0:T(128)S(1)} all-reduce(s32[128]{0:T(128)S(1)} %dynamic-update-slice), channel_id=1, replica_groups=mesh['ctx'=64,'dp'=8] {'ctx'}, use_global_device_ids=true, to_apply=%add | all-reduce | flops 128 | bytes 1024
  43.3 2.5 select_reduce_fusion
  45.9 0.1 iota_add_fusion
  46.0 0.1 add.85
  46.0 0.6 broadcast_compare_fusion
  47.4 106.9 %all-gather.6.cloned.1.call-done = bf16[2048,256]{1,0:T(8,128)(2,1)} async-done(((bf16[32,256]{1,0:T(8,128)(2,1)}), bf16[2048,256]{1,0:T(8,128)(2,1)}) %all-gather.6.cloned.1.call-update) | async-done | bytes 1048592 | tf_op jit(solution)/shard_map/all_gather | solution.py:71
  154.2 1.3 reshape.125
  155.6 138.6 %all-gather.8.cloned.1.call-done = bf16[2048,256]{1,0:T(8,128)(2,1)} async-done(((bf16[32,256]{1,0:T(8,128)(2,1)}), bf16[2048,256]{1,0:T(8,128)(2,1)}) %all-gather.8.cloned.1.call-update) | async-done | bytes 1048592 | tf_op jit(solution)/shard_map/all_gather | solution.py:72
  294.2 1.3 reshape.127
  295.6 0.0 copy-done
  295.6 0.0 copy-done.4
  295.6 1.6 fusion.54
  297.1 146.2 %all-gather.12.cloned.1.call-done = bf16[8192,256]{1,0:T(8,128)(2,1)} async-done(((bf16[128,256]{1,0:T(8,128)(2,1)}), bf16[8192,256]{1,0:T(8,128)(2,1)}) %all-gather.12.cloned.1.call-update) | async-done | bytes 4194320 | tf_op jit(solution)/shard_map/all_gather | solution.py:82
  443.3 6.4 copy.42
  449.8 138.0 %all-gather.10.cloned.1.call-done = bf16[8192,256]{0,1:T(8,128)(2,1)} async-done(((bf16[128,256]{0,1:T(8,128)(2,1)}), bf16[8192,256]{0,1:T(8,128)(2,1)}) %all-gather.10.cloned.1.call-update) | async-done | bytes 4194320 | tf_op jit(solution)/shard_map/all_gather | solution.py:81
  587.8 0.0 copy-start.2
  587.8 4.6 fusion.57
  592.4 0.0 copy-done.2
  592.5 0.2 fusion.28
  592.6 0.0 copy-start.1
  592.6 2.1 fusion.1
  594.8 0.0 copy-done.1
  594.8 0.0 copy-start.6
  594.8 1.8 fusion.15
  596.6 0.0 copy-start.5
  596.6 0.0 copy-start.3
  596.6 0.0 copy-done.6
  596.6 0.6 fusion.23
  597.3 131.5 %all-gather.14.cloned.1.call-done = bf16[4096,256]{1,0:T(8,128)(2,1)} async-done(((bf16[64,256]{1,0:T(8,128)(2,1)}), bf16[4096,256]{1,0:T(8,128)(2,1)}) %all-gather.14.cloned.1.call-update) | async-done | bytes 2097168 | tf_op jit(solution)/shard_map/all_gather | solution.py:99
  728.7 3.4 convolution_convert_fusion
  732.1 0.0 reduce-scatter.2.cloned.1.call-update
  732.1 0.0 copy-done.5
  732.2 44.4 %reduce-scatter.2.cloned.1.call-done = bf16[128,512]{1,0:T(8,128)(2,1)} async-done(((bf16[128,4096]{1,0:T(8,128)(2,1)}), bf16[128,512]{1,0:T(8,128)(2,1)}) %reduce-scatter.2.cloned.1.call-update) | async-done | bytes 131088 | tf_op jit(solution)/shard_map/reduce_scatter | solution.py:104
  776.5 0.0 copy-done.3
  776.5 1.0 multiply_reduce_fusion
  777.6 17.5 %psum.7 = f32[128]{0:T(128)S(1)} all-reduce(f32[128]{0:T(128)S(1)} %multiply_reduce_fusion), channel_id=1, replica_groups=mesh['ctx'=64,'dp'=8] {'dp'}, use_global_device_ids=true, to_apply=%region_7.8 | all-reduce | flops 128 | bytes 1024 | tf_op jit(solution)/shard_map/psum | solution.py:108
  795.0 1.7 multiply_convert_fusion
  (8 shorter events, 0.1 us)
Async XLA Ops:
  6.5 289.0 %copy-start = (bf16[2,4,128,128]{3,2,1,0:T(8,128)(2,1)S(1)}, bf16[2,4,128,128]{3,2,1,0:T(8,128)(2,1)}, u32[]{:S(2)}) copy-start(bf16[2,4,128,128]{3,2,1,0:T(8,128)(2,1)} %param.17) | copy-start | bytes 786436
  6.5 289.0 %copy-start.4 = (bf16[128,256]{1,0:T(8,128)(2,1)S(1)}, bf16[128,256]{1,0:T(8,128)(2,1)}, u32[]{:S(2)}) copy-start(bf16[128,256]{1,0:T(8,128)(2,1)} %param.12) | copy-start | bytes 196612
  6.5 147.7 %all-gather.6.cloned.1.call-start = ((), (), s32[]{:S(2)}) async-start(), calls=%async_computation.1 | async-start | bytes 1064960 | tf_op jit(solution)/shard_map/all_gather | solution.py:71
  7.3 286.9 %all-gather.8.cloned.1.call-start = ((), (), s32[]{:S(2)}) async-start(), calls=%async_computation.2 | async-start | bytes 1064960 | tf_op jit(solution)/shard_map/all_gather | solution.py:72
  8.0 435.3 %all-gather.12.cloned.1.call-start = ((), (), s32[]{:S(2)}) async-start(), calls=%async_computation.4 | async-start | bytes 4259840 | tf_op jit(solution)/shard_map/all_gather | solution.py:82
  8.7 579.0 %all-gather.10.cloned.1.call-start = ((), (), s32[]{:S(2)}) async-start(), calls=%async_computation.3 | async-start | bytes 4259840 | tf_op jit(solution)/shard_map/all_gather | solution.py:81
  10.4 718.3 %all-gather.14.cloned.1.call-start = ((), (), s32[]{:S(2)}) async-start(), calls=%async_computation.5 | async-start | bytes 2129920 | tf_op jit(solution)/shard_map/all_gather | solution.py:99
  11.0 765.6 %reduce-scatter.2.cloned.1.call-start = ((), (), s32[]{:S(2)}) async-start(), calls=%async_computation.6 | async-start | bytes 1179648 | tf_op jit(solution)/shard_map/reduce_scatter | solution.py:104
  587.8 4.7 copy-start.2
  592.6 2.2 copy-start.1
  594.8 1.8 copy-start.6
  596.6 135.5 %copy-start.5 = (bf16[512]{0:T(512)(128)(2,1)S(1)}, bf16[512]{0:T(512)(128)(2,1)}, u32[]{:S(2)}) copy-start(bf16[512]{0:T(512)(128)(2,1)} %param.21) | copy-start | bytes 3076
  596.6 179.9 %copy-start.3 = (bf16[128,512]{1,0:T(8,128)(2,1)S(1)}, bf16[128,512]{1,0:T(8,128)(2,1)}, u32[]{:S(2)}) copy-start(bf16[128,512]{1,0:T(8,128)(2,1)} %param.20) | copy-start | bytes 393220
Sparse Core Ops, SparseCore 0:
  10.6 143.5 all-gather.5
  157.5 136.6 all-gather.7
  297.5 145.7 all-gather.11
  446.2 141.5 all-gather.9
  590.9 137.7 all-gather.13
  732.3 44.2 reduce-scatter.1
where the time goes:
time: 804 us
  waiting for transfers between devices  708 us (88%)
  blocking collectives  46.3 us (6%)
  between operations  14.9 us (2%)
  local copies, waits for them, and re-layouts  13 us (2%)
  matrix products  12 us (1%)
  other arithmetic  8.94 us (1%)
    all_gather x1, waiting for transfers between devices, local(): lax.all_gather(values, 'ctx', axis=0, tiled=True)  146 us
    all_gather x1, waiting for transfers between devices, local(): lax.all_gather(old_values, 'ctx', axis=0, tiled=True)  139 us
    all_gather x1, waiting for transfers between devices, local(): lax.all_gather(keys, 'ctx', axis=0, tiled=True)  138 us
    all_gather x1, waiting for transfers between devices, local(): lax.all_gather(out_proj, 'ctx', axis=0, tiled=True)  131 us
    all_gather x1, waiting for transfers between devices, local(): lax.all_gather(old_keys, 'ctx', axis=0, tiled=True)  107 us
    reduce_scatter x1, waiting for transfers between devices, local(): lax.psum_scatter(partial_sums.astype(jnp.bfloat16), 'dp', scatter_dimensi...  44.4 us
    unnamed x1, blocking collectives  28.8 us
    psum x1, blocking collectives, local(): power = lax.psum(jnp.sum(stream * stream, axis=1), 'dp') / features  17.5 us
  transfers between devices with their start and end apart: 6, of which 6 were waited for; matrix products, arithmetic and copies ran while one was open for 3% of the time, Pallas kernels for 0%

commit v1 on v0

--- a/solution.py
+++ b/solution.py
@@ -96,7 +96,9 @@
     )
     partial_sums = lax.dot_general(
         attn,
-        lax.all_gather(out_proj, "ctx", axis=0, tiled=True),
+        jnp.concatenate(
+            lax.all_to_all(jnp.stack([out_proj] * lax.axis_size("ctx")), "ctx", 0, 0), axis=0
+        ),
         (((1,), (1,)), ((), ())),
         preferred_element_type=jnp.float32,
     )

time: 804 us -> 679 us (0.84)
  waiting for transfers between devices: 708 us -> 481 us
  blocking collectives: 46.3 us -> 125 us
  starting transfers between devices: 0.2 us -> 19 us
    all_gather x1 -> x0, waiting for transfers between devices: 131 us -> none  [local(): lax.all_gather(out_proj, 'ctx', axis=0, tiled=True)]
    all_gather x1, waiting for transfers between devices: 107 us -> 15.8 us  [local(): lax.all_gather(old_keys, 'ctx', axis=0, tiled=True)]
    unnamed x1, blocking collectives: 28.8 us -> 108 us
    all_to_all x0 -> x1, starting transfers between devices: none -> 18.8 us  [local(): lax.all_to_all(jnp.stack([out_proj] * lax.axis_size('ctx')), 'ctx', 0, 0)]
  transfers between devices with their start and end apart: 6 -> 6, of which waited for: 6 -> 5; matrix products, arithmetic and copies ran while one was open for 3% -> 5% of each run, Pallas kernels for 0% -> 0%
where the time goes in v1:
time: 679 us; the launch traced here: 678 us
  waiting for transfers between devices  481 us (71%)
  blocking collectives  125 us (18%)
  starting transfers between devices  19 us (3%)
  local copies, waits for them, and re-layouts  16.3 us (2%)
  between operations  14.6 us (2%)
  matrix products  13.7 us (2%)
  other arithmetic  8.3 us (1%)
    all_gather x1, waiting for transfers between devices, local(): lax.all_gather(values, 'ctx', axis=0, tiled=True)  144 us
    all_gather x1, waiting for transfers between devices, local(): lax.all_gather(keys, 'ctx', axis=0, tiled=True)  138 us
    all_gather x1, waiting for transfers between devices, local(): lax.all_gather(old_values, 'ctx', axis=0, tiled=True)  137 us
    unnamed x1, blocking collectives  108 us
    reduce_scatter x1, waiting for transfers between devices, local(): lax.psum_scatter(partial_sums.astype(jnp.bfloat16), 'dp', scatter_dimensi...  43.7 us
    all_to_all x1, starting transfers between devices, local(): lax.all_to_all(jnp.stack([out_proj] * lax.axis_size('ctx')), 'ctx', 0, 0)  18.8 us
    psum x1, blocking collectives, local(): power = lax.psum(jnp.sum(stream * stream, axis=1), 'dp') / features  17.5 us
    all_gather x1, waiting for transfers between devices, local(): lax.all_gather(old_keys, 'ctx', axis=0, tiled=True)  15.8 us
  transfers between devices with their start and end apart: 6, of which 5 were waited for; matrix products, arithmetic and copies ran while one was open for 5% of the time, Pallas kernels for 0%

profile of v1, /device:TPU:16, one launch (start us, length us, event | category | flops | bytes accessed | tf_op | source)
XLA Modules:
  0.0 678.2 jit_solution(11304450260173666970)
XLA Ops:
  6.5 0.0 copy-start
  6.5 0.0 copy-start.6
  6.5 0.0 all-gather.5.cloned.1.call-start
  6.5 0.7 all-gather.5.cloned.1.call-update
  7.3 0.0 all-gather.7.cloned.1.call-start
  7.3 0.7 all-gather.7.cloned.1.call-update
  8.0 0.0 all-gather.11.cloned.1.call-start
  8.1 0.7 all-gather.11.cloned.1.call-update
  8.7 0.0 all-gather.9.cloned.1.call-start
  8.8 1.6 copy.39
  10.4 0.0 all-gather.9.cloned.1.call-update
  10.4 2.3 stack.2
  12.7 0.0 copy-start.4
  12.7 18.8 %all-to-all-start = ((bf16[64,64,256]{2,1,0:T(8,128)(2,1)}), bf16[64,64,256]{2,1,0:T(8,128)(2,1)S(1)}, u32[]{:S(2)}, u32[]{:S(2)}) async-start(bf16[64,64,256]{2,1,0:T(8,128)(2,1)} %stack.2), calls=%async_computation | async-start | bytes 4194304 | tf_op jit(solution)/shard_map/all_to_all | solution.py:100
  31.6 0.0 reduce-scatter.2.cloned.1.call-start
  31.6 0.0 copy-done.6
  31.7 0.1 iota_add_fusion
  31.7 0.1 add.85
  32.5 1.3 dynamic-slice
  34.5 0.2 dynamic-update-slice
  34.7 107.6 %all-reduce = s32[128]{0:T(128)S(1)} all-reduce(s32[128]{0:T(128)S(1)} %dynamic-update-slice), channel_id=1, replica_groups=mesh['ctx'=64,'dp'=8] {'ctx'}, use_global_device_ids=true, to_apply=%add | all-reduce | flops 128 | bytes 1024
  142.3 2.5 select_reduce_fusion
  144.9 0.6 broadcast_compare_fusion
  145.5 15.8 %all-gather.5.cloned.1.call-done = bf16[2048,256]{1,0:T(8,128)(2,1)} async-done(((bf16[32,256]{1,0:T(8,128)(2,1)}), bf16[2048,256]{1,0:T(8,128)(2,1)}) %all-gather.5.cloned.1.call-update) | async-done | bytes 1048592 | tf_op jit(solution)/shard_map/all_gather | solution.py:71
  161.3 2.1 reshape.130
  163.5 137.3 %all-gather.7.cloned.1.call-done = bf16[2048,256]{1,0:T(8,128)(2,1)} async-done(((bf16[32,256]{1,0:T(8,128)(2,1)}), bf16[2048,256]{1,0:T(8,128)(2,1)}) %all-gather.7.cloned.1.call-update) | async-done | bytes 1048592 | tf_op jit(solution)/shard_map/all_gather | solution.py:72
  300.8 2.2 reshape.132
  302.9 0.0 copy-done
  302.9 0.0 copy-done.4
  302.9 2.8 fusion.54
  305.7 144.2 %all-gather.11.cloned.1.call-done = bf16[8192,256]{1,0:T(8,128)(2,1)} async-done(((bf16[128,256]{1,0:T(8,128)(2,1)}), bf16[8192,256]{1,0:T(8,128)(2,1)}) %all-gather.11.cloned.1.call-update) | async-done | bytes 4194320 | tf_op jit(solution)/shard_map/all_gather | solution.py:82
  449.9 6.3 copy.42
  456.2 138.1 %all-gather.9.cloned.1.call-done = bf16[8192,256]{0,1:T(8,128)(2,1)} async-done(((bf16[128,256]{0,1:T(8,128)(2,1)}), bf16[8192,256]{0,1:T(8,128)(2,1)}) %all-gather.9.cloned.1.call-update) | async-done | bytes 4194320 | tf_op jit(solution)/shard_map/all_gather | solution.py:81
  594.3 0.0 copy-start.2
  594.3 4.6 fusion.57
  599.0 0.0 copy-done.2
  599.0 0.2 fusion.28
  599.2 0.0 copy-start.1
  599.2 2.1 fusion.1
  601.3 0.0 copy-done.1
  601.4 2.5 fusion.15
  603.8 0.0 copy-start.5
  603.8 0.0 copy-start.3
  603.8 2.1 fusion.23
  605.9 0.0 all-to-all-done
  605.9 1.8 convolution_convert_fusion
  607.7 0.0 reduce-scatter.2.cloned.1.call-update
  607.8 0.0 copy-done.5
  607.8 43.7 %reduce-scatter.2.cloned.1.call-done = bf16[128,512]{1,0:T(8,128)(2,1)} async-done(((bf16[128,4096]{1,0:T(8,128)(2,1)}), bf16[128,512]{1,0:T(8,128)(2,1)}) %reduce-scatter.2.cloned.1.call-update) | async-done | bytes 131088 | tf_op jit(solution)/shard_map/reduce_scatter | solution.py:106
  651.5 0.0 copy-done.3
  651.5 1.0 multiply_reduce_fusion
  652.5 17.5 %psum.7 = f32[128]{0:T(128)S(1)} all-reduce(f32[128]{0:T(128)S(1)} %multiply_reduce_fusion), channel_id=1, replica_groups=mesh['ctx'=64,'dp'=8] {'dp'}, use_global_device_ids=true, to_apply=%region_7.8 | all-reduce | flops 128 | bytes 1024 | tf_op jit(solution)/shard_map/psum | solution.py:110
  670.0 1.7 multiply_convert_fusion
  (9 shorter events, 0.1 us)
Async XLA Ops:
  6.5 296.4 %copy-start = (bf16[2,4,128,128]{3,2,1,0:T(8,128)(2,1)S(1)}, bf16[2,4,128,128]{3,2,1,0:T(8,128)(2,1)}, u32[]{:S(2)}) copy-start(bf16[2,4,128,128]{3,2,1,0:T(8,128)(2,1)} %param.17) | copy-start | bytes 786436
  6.5 25.1 %copy-start.6 = (s32[2]{0:T(128)S(1)}, s32[2]{0:T(128)}, u32[]{:S(2)}) copy-start(s32[2]{0:T(128)} %param.22) | copy-start | bytes 28
  6.5 154.8 %all-gather.5.cloned.1.call-start = ((), (), s32[]{:S(2)}) async-start(), calls=%async_computation.2 | async-start | bytes 1064960 | tf_op jit(solution)/shard_map/all_gather | solution.py:71
  7.3 293.5 %all-gather.7.cloned.1.call-start = ((), (), s32[]{:S(2)}) async-start(), calls=%async_computation.3 | async-start | bytes 1064960 | tf_op jit(solution)/shard_map/all_gather | solution.py:72
  8.0 441.9 %all-gather.11.cloned.1.call-start = ((), (), s32[]{:S(2)}) async-start(), calls=%async_computation.5 | async-start | bytes 4259840 | tf_op jit(solution)/shard_map/all_gather | solution.py:82
  8.7 585.6 %all-gather.9.cloned.1.call-start = ((), (), s32[]{:S(2)}) async-start(), calls=%async_computation.4 | async-start | bytes 4259840 | tf_op jit(solution)/shard_map/all_gather | solution.py:81
  12.7 290.2 %copy-start.4 = (bf16[128,256]{1,0:T(8,128)(2,1)S(1)}, bf16[128,256]{1,0:T(8,128)(2,1)}, u32[]{:S(2)}) copy-start(bf16[128,256]{1,0:T(8,128)(2,1)} %param.12) | copy-start | bytes 196612
  12.7 593.2 %all-to-all-start = ((bf16[64,64,256]{2,1,0:T(8,128)(2,1)}), bf16[64,64,256]{2,1,0:T(8,128)(2,1)S(1)}, u32[]{:S(2)}, u32[]{:S(2)}) async-start(bf16[64,64,256]{2,1,0:T(8,128)(2,1)} %stack.2), calls=%async_computation | async-start | bytes 4194304 | tf_op jit(solution)/shard_map/all_to_all | solution.py:100
  31.6 619.9 %reduce-scatter.2.cloned.1.call-start = ((), (), s32[]{:S(2)}) async-start(), calls=%async_computation.6 | async-start | bytes 1179648 | tf_op jit(solution)/shard_map/reduce_scatter | solution.py:106
  594.3 4.7 copy-start.2
  599.2 2.2 copy-start.1
  603.8 3.9 copy-start.5
  603.8 47.7 %copy-start.3 = (bf16[128,512]{1,0:T(8,128)(2,1)S(1)}, bf16[128,512]{1,0:T(8,128)(2,1)}, u32[]{:S(2)}) copy-start(bf16[128,512]{1,0:T(8,128)(2,1)} %param.20) | copy-start | bytes 393220
Sparse Core Ops, SparseCore 0:
  10.6 150.6 all-gather.4
  164.6 136.1 all-gather.6
  304.1 145.7 all-gather.10
  452.7 141.5 all-gather.8
  607.9 43.5 reduce-scatter.1
